TPU v7x, 256 devices: a whole 4x4x8 slice. The times are simulated.
256 devices in a mesh: pts: 128 (over z, y, x), slab: 2 (over core).
Axes of the slice: x: 4, y: 4, z: 8, core: 2. Of those that a mesh axis runs over, the one named last changes fastest.
Arguments:
- features: float32 [65536, 256], P(('slab', 'pts')), parts along dimension 0, may hold values from -25 to 25
- orders: int32 [2, 65536], P(None, ('slab', 'pts')), parts along dimension 1, may hold values from 0 to 32767, as said below
- norm_gains: float32 [2, 2, 256], replicated, may hold values from 0.1 to 1.9
- qkv_weight: bfloat16 [2, 256, 768], replicated, may hold values from -4 to 4
- proj_weight: bfloat16 [2, 256, 256], replicated, may hold values from -0.375 to 0.375
- fc1_weight: bfloat16 [2, 256, 1024], replicated, may hold values from -0.375 to 0.375
- fc2_weight: bfloat16 [2, 1024, 256], replicated, may hold values from -0.1875 to 0.1875
Outputs:
- output_features: float32 [65536, 256], P(('slab', 'pts')), parts along dimension 0
There are 2 independent parts, one for each index of `slab`. A program takes and returns all parts, laid end to end along the dimension named above; an argument that names none is the same for every part. Nothing has to cross between parts.
Inputs may be any that keep to these rules, and one draw needn't show every extreme that they name: `orders`: each row is a permutation of the 32768 storage rows. In each row the 256 serial positions of one device take exactly 1 or 3 of their points from the rows stored on each device, 3 from half of the devices.
All inputs are finite; a program needn't handle non-finite values.
Results may differ from a plain program's by a relative error of at most 0.013.
Values may be sent and summed in bfloat16 or wider, within the bound.
A program may use at most 64 MiB of HBM per device.

v0:
```python
import functools
import math

import jax
import jax.numpy as jnp
from jax import lax
from jax.experimental import pallas as pl
from jax.experimental.pallas import tpu as pltpu
from jax.sharding import PartitionSpec as P

HEADS = 16
PATCH = 1024
HALF = 128
GROUP = 2
UNROLL = 8
SLOTS = 3
F32 = jnp.float32
BF16 = jnp.bfloat16
MESH = pl.DeviceIdType.MESH


def offsets(sizes):
    nz, ny, nx = sizes
    every = [(a, b, c) for a in range(nz) for b in range(ny) for c in range(nx)]

    def hops(o):
        return sum(min(v, n - v) for v, n in zip(o, sizes))

    return sorted((o for o in every if o != (0, 0, 0)), key=lambda o: (-hops(o), o[1], o[2], o[0]))


def iota(shape, dim):
    return lax.broadcasted_iota(jnp.int32, shape, dim)


def one_hot(cond):
    return jnp.where(cond, 1.0, 0.0).astype(BF16)


def mm(a, b):
    return jnp.dot(a, b, preferred_element_type=F32)


def layer_norm(values, gain_row):
    center = values - jnp.mean(values, axis=1, keepdims=True)
    spread = jnp.mean(center * center, axis=1, keepdims=True)
    return center * lax.rsqrt(spread + 1e-05) * gain_row


def stack_halves(rows):
    return jnp.concatenate((rows[:, :HALF], rows[:, HALF:]), axis=0)


def join_halves(stacked):
    count = stacked.shape[0] // 2
    return jnp.concatenate((stacked[:count], stacked[count:]), axis=1)


def kernel(
    sizes, feat_hbm, orders_hbm, gains_hbm, qkv_hbm, proj_hbm, fc1_hbm, fc2_hbm, out_ref,
    feat, orders, gains, qkv_w, proj_w, fc1_w, fc2_w,
    req_send, req_recv, row_send, row_recv, near,
    pick_in, pick_back, pick_out, pick_home, spread, q_buf, k_buf, v_buf, score_a, score_b, totals, peaks, mixed,
    load_sem, self_sem, req_ssem, req_rsem, row_ssem, row_rsem, near_ssem, near_rsem,
):
    nz, ny, nx = sizes
    peers = nz * ny * nx
    rows = feat.shape[0]
    width = 2 * HALF
    slots = SLOTS * peers
    blocks = orders.shape[0]
    me = lax.axis_index("pts")
    zs = [jnp.bitwise_and(jnp.right_shift(me, 4) + i, nz - 1) * (ny * nx) for i in range(nz)]
    ys = [jnp.bitwise_and(jnp.right_shift(me, 2) + i, ny - 1) * nx for i in range(ny)]
    xs = [jnp.bitwise_and(me + i, nx - 1) for i in range(nx)]
    order = offsets(sizes)

    barrier = pltpu.get_barrier_semaphore()

    for a, b, c in order:
        other = zs[a] + ys[b] + xs[c]
        pl.semaphore_signal(barrier, inc=1, device_id={"pts": other}, device_id_type=MESH)

    loads = [
        pltpu.make_async_copy(src, dst, load_sem.at[i])
        for i, (src, dst) in enumerate(
            (
                (orders_hbm, orders), (feat_hbm, feat), (gains_hbm, gains), (qkv_hbm, qkv_w),
                (proj_hbm, proj_w), (fc1_hbm, fc1_w), (fc2_hbm, fc2_w),
            )
        )
    ]
    for load in loads:
        load.start()
    loads[0].wait()

    ri = iota((rows, rows), 0)
    ci = iota((rows, rows), 1)
    keys = []
    left, right = [], []
    for b in range(blocks):
        order_row = orders[b : b + 1, :]
        owner_row = jnp.right_shift(order_row, 8).astype(F32)
        within_row = jnp.bitwise_and(order_row, rows - 1).astype(F32)
        owner_col = jnp.sum(jnp.where(ri == ci, owner_row, 0.0), axis=1, keepdims=True)
        within_col = jnp.sum(jnp.where(ri == ci, within_row, 0.0), axis=1, keepdims=True)
        same = owner_col == owner_row
        rank_col = jnp.sum(jnp.where(same & (ci < ri), 1.0, 0.0), axis=1, keepdims=True)
        rank_row = jnp.sum(jnp.where(same & (ri < ci), 1.0, 0.0), axis=0, keepdims=True)
        keys.append(
            (
                (2.0 * (rank_row * peers + owner_row)).astype(jnp.int32),
                (2.0 * (rank_col * peers + owner_col)).astype(jnp.int32),
            )
        )
        left.append(one_hot(ri == (2.0 * owner_row + b).astype(jnp.int32)))
        lane = iota((rows, HALF), 1)
        right.append(
            jnp.where(rank_col.astype(jnp.int32) == lane, within_col + 1.0, 0.0).astype(BF16)
        )
    request = mm(jnp.concatenate(left, axis=1), jnp.concatenate(right, axis=0))
    req_send.reshape(2 * peers, HALF)[...] = request.astype(BF16)

    pl.semaphore_wait(barrier, peers - 1)

    def to_all(src, dst, ssem, rsem, mine):
        own = pltpu.make_async_copy(src(me), dst(me), mine)
        own.start()
        for a, b, c in order:
            other = zs[a] + ys[b] + xs[c]
            pltpu.make_async_remote_copy(
                src_ref=src(other), dst_ref=dst(me), send_sem=ssem, recv_sem=rsem,
                device_id={"pts": other}, device_id_type=MESH,
            ).start()
        own.wait()

    def all_of(ref, sem):
        pltpu.make_async_copy(ref, ref, sem).wait()

    to_all(lambda i: req_send.at[i], lambda i: req_recv.at[i], req_ssem, req_rsem, self_sem.at[0])

    for b in range(blocks):
        key_row, key_col = keys[b]
        for half in range(2):
            part = pl.ds(half * rows, rows)
            pick_in[b, part, :] = one_hot(iota((rows, 2 * slots), 1) == key_col + half)
            pick_back[b, :, part] = one_hot(iota((2 * slots, rows), 0) == key_row + half)
        spread[b] = one_hot(ri - jnp.bitwise_and(ri, 1) + b == ci)
    for load in loads[1:]:
        load.wait()

    q_buf[0 : 2 * rows, :HALF] = stack_halves(layer_norm(feat[...], gains[0, 0:1, :]).astype(BF16))
    all_of(req_recv.at[pl.ds(0, peers - 1)], req_rsem)
    asked = req_recv.reshape(2 * peers, HALF)[...]

    def selections(b):
        wanted = mm(spread[b], asked)
        parity = jnp.bitwise_and(iota(wanted.shape, 0), 1).astype(F32)
        wanted = jnp.where(wanted > 0.5, wanted - 1.0 + rows * parity, -4.0)
        return wanted

    def fill_out(b, wanted):
        for j in range(SLOTS):
            col = wanted[:, j : j + 1].astype(jnp.int32)
            pick_out[b, pl.ds(j * 2 * peers, 2 * peers), :] = one_hot(iota((2 * peers, 2 * rows), 1) == col)

    def fill_home(b, wanted):
        flat = wanted.T.astype(jnp.int32)
        for j in range(SLOTS):
            pick_home[b, :, pl.ds(j * 2 * peers, 2 * peers)] = one_hot(
                iota((2 * rows, 2 * peers), 0) == flat[j : j + 1, :]
            )

    def ship(phase, values):
        row_send.at[phase].reshape(2 * slots, HALF)[...] = values.astype(BF16)
        to_all(
            lambda i: row_send.at[phase, :, i], lambda i: row_recv.at[phase, :, i],
            row_ssem.at[phase], row_rsem.at[phase], self_sem.at[1 + phase],
        )

    def landed(phase):
        all_of(row_recv.at[phase, :, pl.ds(0, peers - 1)], row_rsem.at[phase])
        return row_recv.at[phase].reshape(2 * slots, HALF)[...]

    wanted0 = selections(0)
    fill_out(0, wanted0)
    ship(0, mm(pick_out[0], q_buf[0 : 2 * rows, :HALF]))

    fill_home(0, wanted0)
    wanted1 = selections(1)
    fill_out(1, wanted1)
    fill_home(1, wanted1)

    scale = (width // HEADS) ** (-0.5) * math.log2(math.e)
    half_rows = rows // 2
    top, bottom = pl.ds(0, half_rows), pl.ds(half_rows, half_rows)
    near_copies = []
    for b in range(blocks):
        near[b, 0] = join_halves(mm(pick_in[b], landed(2 * b))).astype(BF16)

        def pass_on(index, source, slot, part, step):
            copy = pltpu.make_async_remote_copy(
                src_ref=near.at[b, source, part], dst_ref=near.at[b, slot, part],
                send_sem=near_ssem.at[b, index], recv_sem=near_rsem.at[b, index],
                device_id={"pts": me - xs[0] + xs[step]}, device_id_type=MESH,
            )
            copy.start()
            near_copies.append(copy)
            return copy

        up_top = pass_on(0, 0, 1, top, 1)
        down_bottom = pass_on(1, 0, 3, bottom, 3)
        up_bottom = pass_on(2, 0, 1, bottom, 1)
        down_top = pass_on(3, 0, 3, top, 3)

        def keep(at, pair):
            k_buf[pl.ds(at * rows, rows), :] = pair[:, :width].astype(BF16)
            values = pair[:, width:].astype(BF16)
            ones = jnp.ones((rows, HALF), BF16)
            for half in range(2):
                v_buf[half, pl.ds(at * rows, rows), :] = jnp.concatenate(
                    (values[:, half * HALF : (half + 1) * HALF], ones), axis=1
                )

        def attend(at, first, last):
            keys = pl.ds(at * rows, rows)
            count = GROUP * rows

            def part_of(i):
                return pl.ds(pl.multiple_of(i * count, count), count)

            def score(i, into):
                into[...] = lax.dot_general(
                    q_buf[part_of(i), :], k_buf[keys, :], (((1,), (1,)), ((), ())),
                    preferred_element_type=F32,
                )

            def absorb(i, scores_ref):
                part = part_of(i)
                group = i * GROUP // (HEADS // 2)
                scores = scores_ref[...]
                low, high = scores[:, :HALF], scores[:, HALF:]
                peak = jnp.broadcast_to(
                    jnp.max(jnp.maximum(low, high), axis=1, keepdims=True), (count, HALF)
                )
                if not first:
                    before = peaks[part, :]
                    peak = jnp.maximum(before, peak)
                    decay = jnp.exp2(before - peak)
                if not last:
                    peaks[part, :] = peak
                weights = jnp.exp2(
                    jnp.concatenate(((low - peak).astype(BF16), (high - peak).astype(BF16)), axis=1)
                )
                both = mm(weights, v_buf[group, keys, :])
                tops, sums = both[:, :HALF], both[:, HALF:]
                if not first:
                    tops = tops + totals[part, :HALF] * decay
                    sums = sums + totals[part, HALF:] * decay
                if not last:
                    totals[part, :HALF] = tops
                    totals[part, HALF:] = sums
                else:
                    result = tops / sums
                    owner = jnp.right_shift(iota((rows, HALF), 1), 4)
                    within = GROUP * i % (HEADS // 2)
                    merged = mixed[group]
                    for g in range(GROUP):
                        merged = jnp.where(owner == within + g, result[g * rows : (g + 1) * rows], merged)
                    mixed[group] = merged

            steps = HEADS // GROUP
            score(0, score_a)

            def some(ii, carry):
                for u in range(0, UNROLL, 2):
                    i = ii * UNROLL + u
                    score(i + 1, score_b)
                    absorb(i, score_a)
                    score((i + 2) % steps, score_a)
                    absorb(i + 1, score_b)
                return carry

            lax.fori_loop(0, steps // UNROLL, some, 0)

        projected = mm(near[b, 0], qkv_w[b])
        queries = (projected[:, :width] * scale).astype(BF16)
        for h in range(HEADS):
            q_buf[pl.ds(h * rows, rows), :] = queries * one_hot(jnp.right_shift(iota((1, width), 1), 4) == h)
        keep(0, projected[:, width:])
        attend(0, True, False)

        up_top.wait_recv()
        far_top = pass_on(4, 1, 2, top, 1)
        down_bottom.wait_recv()
        far_bottom = pass_on(5, 3, 2, bottom, 3)
        def others(at, block):
            keep(at, mm(block, qkv_w[b, :, width:]))

        others(1, jnp.concatenate((near[b, 1, top], near[b, 3, bottom]), axis=0))
        attend(1, False, False)
        up_bottom.wait_recv()
        down_top.wait_recv()
        others(2, jnp.concatenate((near[b, 3, top], near[b, 1, bottom]), axis=0))
        attend(2, False, False)
        far_top.wait_recv()
        far_bottom.wait_recv()
        others(3, near[b, 2])
        attend(3, False, True)
        heads = jnp.concatenate((mixed[0], mixed[1]), axis=1).astype(BF16)
        branch = mm(heads, proj_w[b]).astype(BF16)
        ship(2 * b + 1, mm(pick_back[b], stack_halves(branch)))

        attended = feat[...] + join_halves(mm(pick_home[b], landed(2 * b + 1)))
        normed_two = layer_norm(attended, gains[b, 1:2, :]).astype(BF16)
        hidden = mm(normed_two, fc1_w[b])
        expanded = (0.5 * hidden * (1.0 + lax.erf(hidden * (0.5**0.5)))).astype(BF16)
        state = attended + mm(expanded, fc2_w[b])
        if b + 1 < blocks:
            normed = layer_norm(state, gains[b + 1, 0:1, :]).astype(BF16)
            ship(2 * b + 2, mm(pick_out[b + 1], stack_halves(normed)))
            feat[...] = state
        else:
            out_ref[...] = state

    all_of(req_send.at[pl.ds(0, peers - 1)], req_ssem)
    for phase in range(2 * blocks):
        all_of(row_send.at[phase, :, pl.ds(0, peers - 1)], row_ssem.at[phase])
    for copy in near_copies:
        copy.wait_send()


def local(sizes, features, orders, norm_gains, qkv_weight, proj_weight, fc1_weight, fc2_weight):
    rows, width = features.shape
    peers = math.prod(sizes)
    blocks = orders.shape[0]
    args = (features, orders, norm_gains, qkv_weight, proj_weight, fc1_weight, fc2_weight)
    slots = SLOTS * peers
    return pl.pallas_call(
        functools.partial(kernel, sizes),
        out_shape=jax.ShapeDtypeStruct((rows, width), F32),
        in_specs=[pl.BlockSpec(memory_space=pl.ANY)] * len(args),
        out_specs=pl.BlockSpec(memory_space=pltpu.VMEM),
        scratch_shapes=[pltpu.VMEM(a.shape, a.dtype) for a in args]
        + [
            pltpu.VMEM((peers, 2, HALF), BF16),
            pltpu.VMEM((peers, 2, HALF), BF16),
            pltpu.VMEM((2 * blocks, SLOTS, peers, 2, HALF), BF16),
            pltpu.VMEM((2 * blocks, SLOTS, peers, 2, HALF), BF16),
            pltpu.VMEM((blocks, PATCH // rows, rows, width), BF16),
            pltpu.VMEM((blocks, 2 * rows, 2 * slots), BF16),
            pltpu.VMEM((blocks, 2 * slots, 2 * rows), BF16),
            pltpu.VMEM((blocks, 2 * slots, 2 * rows), BF16),
            pltpu.VMEM((blocks, 2 * rows, 2 * slots), BF16),
            pltpu.VMEM((blocks, rows, rows), BF16),
            pltpu.VMEM((HEADS * rows, width), BF16),
            pltpu.VMEM((PATCH, width), BF16),
            pltpu.VMEM((2, PATCH, width), BF16),
            pltpu.VMEM((GROUP * rows, rows), F32),
            pltpu.VMEM((GROUP * rows, rows), F32),
            pltpu.VMEM((HEADS * rows, width), F32),
            pltpu.VMEM((HEADS * rows, HALF), F32),
            pltpu.VMEM((2, rows, HALF), F32),
            pltpu.SemaphoreType.DMA((len(args),)),
            pltpu.SemaphoreType.DMA((1 + 2 * blocks,)),
            pltpu.SemaphoreType.DMA,
            pltpu.SemaphoreType.DMA,
            pltpu.SemaphoreType.DMA((2 * blocks,)),
            pltpu.SemaphoreType.DMA((2 * blocks,)),
            pltpu.SemaphoreType.DMA((blocks, 6)),
            pltpu.SemaphoreType.DMA((blocks, 6)),
        ],
        compiler_params=pltpu.CompilerParams(collective_id=0, has_side_effects=True),
    )(*args)


def solution(mesh):
    sizes = (8, 4, 4)
    placed = (P(("slab", "pts"), None), P(None, ("slab", "pts")), P(), P(), P(), P(), P())
    return jax.shard_map(
        functools.partial(local, sizes),
        mesh=mesh,
        in_specs=placed,
        out_specs=P(("slab", "pts"), None),
        check_vma=False,
    )
```

profile of v0, /device:TPU:2, one launch (start us, length us, event | category | flops | bytes accessed | tf_op | source)
XLA Modules:
  0.0 75.6 jit_solution(15098260745491889221)
XLA Ops:
  0.0 73.9 %shard_map.73 = f32[256,256]{1,0:T(8,128)} custom-call(f32[256,256]{1,0:T(8,128)} %feat_hbm.1, s32[2,256]{1,0:T(2,128)} %orders_hbm.1, f32[2,2,256]{2,1,0:T(2,128)} %gains_hbm.1, bf16[2,256,768]{2,1,0:T(8,128)(2,1)} %qkv_hbm.1, bf16[2,256,256]{2,1,0:T(8,128)(2,1)} %proj_hbm.1, bf16[2,256,1024]{2,1,0:T(8,128)(2,1)} %fc1_hbm.1, bf16[2,1024,256]{2,1,0:T(8,128)(2,1)} %fc2_hbm.1), custom_call_target="tpu_custom_call" | custom-call | tf_op jit(solution)/shard_map/pallas_call | solution.py:339
  73.9 1.7 %copy.9 = f32[256,256]{1,0:T(8,128)} copy(f32[256,256]{1,0:T(8,128)} %shard_map.73) | data formatting | bytes 524288
where the time goes:
time: 75.8 us; the launch traced here: 75.6 us
  Pallas kernels  73.9 us (97%)
  local copies, waits for them, and re-layouts  1.67 us (2%)
    pallas_call x1, Pallas kernels, local(): pl.pallas_call(functools.partial(kernel, sizes), out_shape=jax.ShapeDtype...  73.9 us
    unnamed x1, local copies, waits for them, and re-layouts  1.67 us

commit v1 on v0

--- a/solution.py
+++ b/solution.py
@@ -12,7 +12,6 @@
 PATCH = 1024
 HALF = 128
 GROUP = 2
-UNROLL = 8
 SLOTS = 3
 F32 = jnp.float32
 BF16 = jnp.bfloat16
@@ -39,6 +38,12 @@
 
 def mm(a, b):
     return jnp.dot(a, b, preferred_element_type=F32)
+
+
+def move_rows(picks, b, rows):
+    count = picks.shape[1] // 2
+    parts = [mm(picks[b, i * count : (i + 1) * count, :], rows) for i in range(2)]
+    return jnp.concatenate(parts, axis=0)
 
 
 def layer_norm(values, gain_row):
@@ -149,7 +154,7 @@
     for load in loads[1:]:
         load.wait()
 
-    q_buf[0 : 2 * rows, :HALF] = stack_halves(layer_norm(feat[...], gains[0, 0:1, :]).astype(BF16))
+    q_buf[0 : 2 * rows, :] = stack_halves(layer_norm(feat[...], gains[0, 0:1, :]).astype(BF16))
     all_of(req_recv.at[pl.ds(0, peers - 1)], req_rsem)
     asked = req_recv.reshape(2 * peers, HALF)[...]
 
@@ -184,7 +189,7 @@
 
     wanted0 = selections(0)
     fill_out(0, wanted0)
-    ship(0, mm(pick_out[0], q_buf[0 : 2 * rows, :HALF]))
+    ship(0, move_rows(pick_out, 0, q_buf[0 : 2 * rows, :]))
 
     fill_home(0, wanted0)
     wanted1 = selections(1)
@@ -196,7 +201,7 @@
     top, bottom = pl.ds(0, half_rows), pl.ds(half_rows, half_rows)
     near_copies = []
     for b in range(blocks):
-        near[b, 0] = join_halves(mm(pick_in[b], landed(2 * b))).astype(BF16)
+        near[b, 0] = join_halves(move_rows(pick_in, b, landed(2 * b))).astype(BF16)
 
         def pass_on(index, source, slot, part, step):
             copy = pltpu.make_async_remote_copy(
@@ -214,7 +219,8 @@
         down_top = pass_on(3, 0, 3, top, 3)
 
         def keep(at, pair):
-            k_buf[pl.ds(at * rows, rows), :] = pair[:, :width].astype(BF16)
+            for half in range(2):
+                k_buf[half, pl.ds(at * rows, rows), :] = pair[:, half * HALF : (half + 1) * HALF].astype(BF16)
             values = pair[:, width:].astype(BF16)
             ones = jnp.ones((rows, HALF), BF16)
             for half in range(2):
@@ -227,12 +233,12 @@
             count = GROUP * rows
 
             def part_of(i):
-                return pl.ds(pl.multiple_of(i * count, count), count)
+                return pl.ds(i * count, count)
 
             def score(i, into):
                 into[...] = lax.dot_general(
-                    q_buf[part_of(i), :], k_buf[keys, :], (((1,), (1,)), ((), ())),
-                    preferred_element_type=F32,
+                    q_buf[part_of(i), :], k_buf[i * GROUP // (HEADS // 2), keys, :],
+                    (((1,), (1,)), ((), ())), preferred_element_type=F32,
                 )
 
             def absorb(i, scores_ref):
@@ -272,21 +278,19 @@
             steps = HEADS // GROUP
             score(0, score_a)
 
-            def some(ii, carry):
-                for u in range(0, UNROLL, 2):
-                    i = ii * UNROLL + u
-                    score(i + 1, score_b)
-                    absorb(i, score_a)
-                    score((i + 2) % steps, score_a)
-                    absorb(i + 1, score_b)
-                return carry
-
-            lax.fori_loop(0, steps // UNROLL, some, 0)
+            for i in range(0, steps, 2):
+                score(i + 1, score_b)
+                absorb(i, score_a)
+                if i + 2 < steps:
+                    score(i + 2, score_a)
+                absorb(i + 1, score_b)
 
         projected = mm(near[b, 0], qkv_w[b])
         queries = (projected[:, :width] * scale).astype(BF16)
         for h in range(HEADS):
-            q_buf[pl.ds(h * rows, rows), :] = queries * one_hot(jnp.right_shift(iota((1, width), 1), 4) == h)
+            half = h // (HEADS // 2)
+            mask = one_hot(jnp.right_shift(iota((1, HALF), 1), 4) == h % (HEADS // 2))
+            q_buf[pl.ds(h * rows, rows), :] = queries[:, half * HALF : (half + 1) * HALF] * mask
         keep(0, projected[:, width:])
         attend(0, True, False)
 
@@ -309,16 +313,16 @@
         attend(3, False, True)
         heads = jnp.concatenate((mixed[0], mixed[1]), axis=1).astype(BF16)
         branch = mm(heads, proj_w[b]).astype(BF16)
-        ship(2 * b + 1, mm(pick_back[b], stack_halves(branch)))
-
-        attended = feat[...] + join_halves(mm(pick_home[b], landed(2 * b + 1)))
+        ship(2 * b + 1, move_rows(pick_back, b, stack_halves(branch)))
+
+        attended = feat[...] + join_halves(move_rows(pick_home, b, landed(2 * b + 1)))
         normed_two = layer_norm(attended, gains[b, 1:2, :]).astype(BF16)
         hidden = mm(normed_two, fc1_w[b])
         expanded = (0.5 * hidden * (1.0 + lax.erf(hidden * (0.5**0.5)))).astype(BF16)
         state = attended + mm(expanded, fc2_w[b])
         if b + 1 < blocks:
             normed = layer_norm(state, gains[b + 1, 0:1, :]).astype(BF16)
-            ship(2 * b + 2, mm(pick_out[b + 1], stack_halves(normed)))
+            ship(2 * b + 2, move_rows(pick_out, b + 1, stack_halves(normed)))
             feat[...] = state
         else:
             out_ref[...] = state
@@ -353,8 +357,8 @@
             pltpu.VMEM((blocks, 2 * slots, 2 * rows), BF16),
             pltpu.VMEM((blocks, 2 * rows, 2 * slots), BF16),
             pltpu.VMEM((blocks, rows, rows), BF16),
-            pltpu.VMEM((HEADS * rows, width), BF16),
-            pltpu.VMEM((PATCH, width), BF16),
+            pltpu.VMEM((HEADS * rows, HALF), BF16),
+            pltpu.VMEM((2, PATCH, HALF), BF16),
             pltpu.VMEM((2, PATCH, width), BF16),
             pltpu.VMEM((GROUP * rows, rows), F32),
             pltpu.VMEM((GROUP * rows, rows), F32),

time: 75.8 us -> 74.6 us (0.984)
  Pallas kernels: 73.9 us -> 72.8 us
    pallas_call x1, Pallas kernels: 73.9 us -> 72.8 us  [local(): pl.pallas_call(functools.partial(kernel, sizes), out_shape=jax.ShapeDtype...]
where the time goes in v1:
time: 74.6 us; the launch traced here: 74.5 us
  Pallas kernels  72.8 us (98%)
  local copies, waits for them, and re-layouts  1.67 us (2%)
    pallas_call x1, Pallas kernels, local(): pl.pallas_call(functools.partial(kernel, sizes), out_shape=jax.ShapeDtype...  72.8 us
    unnamed x1, local copies, waits for them, and re-layouts  1.67 us

profile of v1, /device:TPU:2, one launch (start us, length us, event | category | flops | bytes accessed | tf_op | source)
XLA Modules:
  0.0 74.5 jit_solution(5271668018623729959)
XLA Ops:
  0.0 72.8 %shard_map.73 = f32[256,256]{1,0:T(8,128)} custom-call(f32[256,256]{1,0:T(8,128)} %feat_hbm.1, s32[2,256]{1,0:T(2,128)} %orders_hbm.1, f32[2,2,256]{2,1,0:T(2,128)} %gains_hbm.1, bf16[2,256,768]{2,1,0:T(8,128)(2,1)} %qkv_hbm.1, bf16[2,256,256]{2,1,0:T(8,128)(2,1)} %proj_hbm.1, bf16[2,256,1024]{2,1,0:T(8,128)(2,1)} %fc1_hbm.1, bf16[2,1024,256]{2,1,0:T(8,128)(2,1)} %fc2_hbm.1), custom_call_target="tpu_custom_call" | custom-call | tf_op jit(solution)/shard_map/pallas_call | solution.py:343
  72.8 1.7 %copy.9 = f32[256,256]{1,0:T(8,128)} copy(f32[256,256]{1,0:T(8,128)} %shard_map.73) | data formatting | bytes 524288

commit v2 on v1

--- a/solution.py
+++ b/solution.py
@@ -197,8 +197,8 @@
     fill_home(1, wanted1)
 
     scale = (width // HEADS) ** (-0.5) * math.log2(math.e)
-    half_rows = rows // 2
-    top, bottom = pl.ds(0, half_rows), pl.ds(half_rows, half_rows)
+    direct = rows * 5 // 8
+    top, bottom = pl.ds(0, direct), pl.ds(direct, rows - direct)
     near_copies = []
     for b in range(blocks):
         near[b, 0] = join_halves(move_rows(pick_in, b, landed(2 * b))).astype(BF16)
@@ -213,9 +213,10 @@
             near_copies.append(copy)
             return copy
 
+        down_bottom = pass_on(1, 0, 3, bottom, 3)
         up_top = pass_on(0, 0, 1, top, 1)
-        down_bottom = pass_on(1, 0, 3, bottom, 3)
         up_bottom = pass_on(2, 0, 1, bottom, 1)
+        far_top = pass_on(4, 0, 2, top, 2)
         down_top = pass_on(3, 0, 3, top, 3)
 
         def keep(at, pair):
@@ -294,10 +295,9 @@
         keep(0, projected[:, width:])
         attend(0, True, False)
 
-        up_top.wait_recv()
-        far_top = pass_on(4, 1, 2, top, 1)
         down_bottom.wait_recv()
         far_bottom = pass_on(5, 3, 2, bottom, 3)
+        up_top.wait_recv()
         def others(at, block):
             keep(at, mm(block, qkv_w[b, :, width:]))
 
@@ -342,7 +342,7 @@
     slots = SLOTS * peers
     return pl.pallas_call(
         functools.partial(kernel, sizes),
-        out_shape=jax.ShapeDtypeStruct((rows, width), F32),
+        out_shape=pltpu.VMEM((rows, width), F32),
         in_specs=[pl.BlockSpec(memory_space=pl.ANY)] * len(args),
         out_specs=pl.BlockSpec(memory_space=pltpu.VMEM),
         scratch_shapes=[pltpu.VMEM(a.shape, a.dtype) for a in args]

time: 74.6 us -> 72.5 us (0.972)
  Pallas kernels: 72.8 us -> 71.7 us
  local copies, waits for them, and re-layouts: 1.67 us -> 0.71 us
    pallas_call x1, Pallas kernels: 72.8 us -> 71.7 us  [local(): pl.pallas_call(functools.partial(kernel, sizes), out_shape=pltpu.VMEM((ro...]
    unnamed x1, local copies, waits for them, and re-layouts: 1.67 us -> 0.71 us
where the time goes in v2:
time: 72.5 us; the launch traced here: 72.4 us
  Pallas kernels  71.7 us (99%)
    pallas_call x1, Pallas kernels, local(): pl.pallas_call(functools.partial(kernel, sizes), out_shape=pltpu.VMEM((ro...  71.7 us

profile of v2, /device:TPU:2, one launch (start us, length us, event | category | flops | bytes accessed | tf_op | source)
XLA Modules:
  0.0 72.4 jit_solution(4342493285226843163)
XLA Ops:
  0.0 71.7 %shard_map.73 = f32[256,256]{1,0:T(8,128)S(1)} custom-call(f32[256,256]{1,0:T(8,128)} %feat_hbm.1, s32[2,256]{1,0:T(2,128)} %orders_hbm.1, f32[2,2,256]{2,1,0:T(2,128)} %gains_hbm.1, bf16[2,256,768]{2,1,0:T(8,128)(2,1)} %qkv_hbm.1, bf16[2,256,256]{2,1,0:T(8,128)(2,1)} %proj_hbm.1, bf16[2,256,1024]{2,1,0:T(8,128)(2,1)} %fc1_hbm.1, bf16[2,1024,256]{2,1,0:T(8,128)(2,1)} %fc2_hbm.1), custom_call_target="tpu_custom_call" | custom-call | tf_op jit(solution)/shard_map/pallas_call | solution.py:343
  71.7 0.7 copy.9

commit v3 on v2

--- a/solution.py
+++ b/solution.py
@@ -142,7 +142,7 @@
     def all_of(ref, sem):
         pltpu.make_async_copy(ref, ref, sem).wait()
 
-    to_all(lambda i: req_send.at[i], lambda i: req_recv.at[i], req_ssem, req_rsem, self_sem.at[0])
+    to_all(lambda i: req_send.at[i], lambda i: req_recv.at[i], req_ssem, req_rsem, self_sem)
 
     for b in range(blocks):
         key_row, key_col = keys[b]
@@ -180,7 +180,7 @@
         row_send.at[phase].reshape(2 * slots, HALF)[...] = values.astype(BF16)
         to_all(
             lambda i: row_send.at[phase, :, i], lambda i: row_recv.at[phase, :, i],
-            row_ssem.at[phase], row_rsem.at[phase], self_sem.at[1 + phase],
+            row_ssem, row_rsem.at[phase], self_sem,
         )
 
     def landed(phase):
@@ -197,20 +197,18 @@
     fill_home(1, wanted1)
 
     scale = (width // HEADS) ** (-0.5) * math.log2(math.e)
-    direct = rows * 5 // 8
+    direct = rows * 3 // 4
     top, bottom = pl.ds(0, direct), pl.ds(direct, rows - direct)
-    near_copies = []
     for b in range(blocks):
         near[b, 0] = join_halves(move_rows(pick_in, b, landed(2 * b))).astype(BF16)
 
         def pass_on(index, source, slot, part, step):
             copy = pltpu.make_async_remote_copy(
                 src_ref=near.at[b, source, part], dst_ref=near.at[b, slot, part],
-                send_sem=near_ssem.at[b, index], recv_sem=near_rsem.at[b, index],
+                send_sem=near_ssem, recv_sem=near_rsem.at[b, index],
                 device_id={"pts": me - xs[0] + xs[step]}, device_id_type=MESH,
             )
             copy.start()
-            near_copies.append(copy)
             return copy
 
         down_bottom = pass_on(1, 0, 3, bottom, 3)
@@ -219,13 +217,14 @@
         far_top = pass_on(4, 0, 2, top, 2)
         down_top = pass_on(3, 0, 3, top, 3)
 
-        def keep(at, pair):
+        def keep(at, pair, start=0):
+            part = pl.ds(at * rows + start, pair.shape[0])
             for half in range(2):
-                k_buf[half, pl.ds(at * rows, rows), :] = pair[:, half * HALF : (half + 1) * HALF].astype(BF16)
+                k_buf[half, part, :] = pair[:, half * HALF : (half + 1) * HALF].astype(BF16)
             values = pair[:, width:].astype(BF16)
-            ones = jnp.ones((rows, HALF), BF16)
+            ones = jnp.ones((pair.shape[0], HALF), BF16)
             for half in range(2):
-                v_buf[half, pl.ds(at * rows, rows), :] = jnp.concatenate(
+                v_buf[half, part, :] = jnp.concatenate(
                     (values[:, half * HALF : (half + 1) * HALF], ones), axis=1
                 )
 
@@ -298,8 +297,8 @@
         down_bottom.wait_recv()
         far_bottom = pass_on(5, 3, 2, bottom, 3)
         up_top.wait_recv()
-        def others(at, block):
-            keep(at, mm(block, qkv_w[b, :, width:]))
+        def others(at, block, start=0):
+            keep(at, mm(block, qkv_w[b, :, width:]), start)
 
         others(1, jnp.concatenate((near[b, 1, top], near[b, 3, bottom]), axis=0))
         attend(1, False, False)
@@ -308,8 +307,9 @@
         others(2, jnp.concatenate((near[b, 3, top], near[b, 1, bottom]), axis=0))
         attend(2, False, False)
         far_top.wait_recv()
+        others(3, near[b, 2, top])
         far_bottom.wait_recv()
-        others(3, near[b, 2])
+        others(3, near[b, 2, bottom], direct)
         attend(3, False, True)
         heads = jnp.concatenate((mixed[0], mixed[1]), axis=1).astype(BF16)
         branch = mm(heads, proj_w[b]).astype(BF16)
@@ -328,10 +328,8 @@
             out_ref[...] = state
 
     all_of(req_send.at[pl.ds(0, peers - 1)], req_ssem)
-    for phase in range(2 * blocks):
-        all_of(row_send.at[phase, :, pl.ds(0, peers - 1)], row_ssem.at[phase])
-    for copy in near_copies:
-        copy.wait_send()
+    all_of(row_send.at[:, :, pl.ds(0, peers - 1)], row_ssem)
+    all_of(near.at[:, pl.ds(0, PATCH // rows - 1)], near_ssem)
 
 
 def local(sizes, features, orders, norm_gains, qkv_weight, proj_weight, fc1_weight, fc2_weight):
@@ -366,12 +364,12 @@
             pltpu.VMEM((HEADS * rows, HALF), F32),
             pltpu.VMEM((2, rows, HALF), F32),
             pltpu.SemaphoreType.DMA((len(args),)),
-            pltpu.SemaphoreType.DMA((1 + 2 * blocks,)),
+            pltpu.SemaphoreType.DMA,
+            pltpu.SemaphoreType.DMA,
             pltpu.SemaphoreType.DMA,
             pltpu.SemaphoreType.DMA,
             pltpu.SemaphoreType.DMA((2 * blocks,)),
-            pltpu.SemaphoreType.DMA((2 * blocks,)),
-            pltpu.SemaphoreType.DMA((blocks, 6)),
+            pltpu.SemaphoreType.DMA,
             pltpu.SemaphoreType.DMA((blocks, 6)),
         ],
         compiler_params=pltpu.CompilerParams(collective_id=0, has_side_effects=True),

time: 72.5 us -> 72.8 us (level)
  no operation moved by 1% of the time
where the time goes in v3:
time: 72.8 us; the launch traced here: 72.7 us
  Pallas kernels  72 us (99%)
    pallas_call x1, Pallas kernels, local(): pl.pallas_call(functools.partial(kernel, sizes), out_shape=pltpu.VMEM((ro...  72 us

profile of v3, /device:TPU:2, one launch (start us, length us, event | category | flops | bytes accessed | tf_op | source)
XLA Modules:
  0.0 72.7 jit_solution(15520700258270146843)
XLA Ops:
  0.0 72.0 %shard_map.73 = f32[256,256]{1,0:T(8,128)S(1)} custom-call(f32[256,256]{1,0:T(8,128)} %feat_hbm.1, s32[2,256]{1,0:T(2,128)} %orders_hbm.1, f32[2,2,256]{2,1,0:T(2,128)} %gains_hbm.1, bf16[2,256,768]{2,1,0:T(8,128)(2,1)} %qkv_hbm.1, bf16[2,256,256]{2,1,0:T(8,128)(2,1)} %proj_hbm.1, bf16[2,256,1024]{2,1,0:T(8,128)(2,1)} %fc1_hbm.1, bf16[2,1024,256]{2,1,0:T(8,128)(2,1)} %fc2_hbm.1), custom_call_target="tpu_custom_call" | custom-call | tf_op jit(solution)/shard_map/pallas_call | solution.py:341
  72.0 0.7 copy.9
